TPU v7x, 512 devices: a whole 4x8x8 slice. The times are simulated.
512 devices in a mesh: ctx: 32 (over x, z_hi, core), tp: 16 (over y, z_lo).
Axes of the slice: x: 4, y: 8, z: 8 (z_hi: 4, z_lo: 2; z = z_hi * 2 + z_lo), core: 2. Of those that a mesh axis runs over, the one named last changes fastest.
Arguments:
- queries: bfloat16 [8192, 2048], P('ctx', 'tp'), may hold values from -24 to 24
- key_heads: bfloat16 [8192, 4, 128], P('ctx'), may hold values from -6 to 6
- head_values: bfloat16 [8192, 4, 128], P('ctx'), may hold values from -6 to 6
- hidden: bfloat16 [8192, 4096], P('ctx'), may hold values from -0.59765625 to 0.59765625
- out_proj: bfloat16 [2048, 4096], P('tp'), may hold values from -0.125 to 0.125
- norm_gain: float32 [4096], replicated, may hold values from 0.25 to 1.75
- x_proj: bfloat16 [4096, 4096], P('ctx', 'tp'), may hold values from -0.046875 to 0.046875
- bc_proj: bfloat16 [4096, 4, 256], P('ctx'), may hold values from -0.09375 to 0.09375
- dt_proj: bfloat16 [4096, 64], P('ctx', 'tp'), may hold values from -0.09375 to 0.09375
- dt_bias: float32 [64], P('tp'), may hold values from -12 to 0
- decay_log: float32 [64], P('tp'), may hold values from -10 to 3
- skip_gain: float32 [64], P('tp'), may hold values from 0.5 to 1.5
Outputs:
- residual_out: bfloat16 [8192, 4096], P('ctx', 'tp')
- mamba_out: bfloat16 [8192, 4096], P('ctx', 'tp')
All inputs are finite; a program needn't handle non-finite values.
Results may differ from a plain program's by a relative error of at most 0.034.
Values may be sent and summed in bfloat16 or wider, within the bound.
No kernel may reach another device: no remote copies, remote signals or barrier semaphores. Data moves between devices by JAX's collectives and lax.ppermute only.
A program may use at most 64 MiB of HBM per device.

v0:
```python
import math
import jax
import jax.numpy as jnp
from jax import lax
from jax.sharding import PartitionSpec as P


def prefix(value, axis, join, neutral, backward):
    count, mine = (lax.axis_size(axis), lax.axis_index(axis))
    pieces = jax.tree.map(lambda part: lax.all_gather(part, axis), value)
    if backward:
        pieces = jax.tree.map(lambda part: part[::-1], pieces)
        mine = count - 1 - mine
    so_far = jax.tree.map(
        lambda part, zero: jnp.full_like(part, 0) + jnp.asarray(zero, part.dtype), value, neutral
    )

    def lap(position, so_far):
        longer = join(so_far, jax.tree.map(lambda part: part[position], pieces))
        return jax.tree.map(lambda new, old: jnp.where(position < mine, new, old), longer, so_far)

    return lax.fori_loop(0, count - 1, lap, so_far)


def chain(earlier, later):
    return (earlier[0] * later[0], later[0][..., None, None] * earlier[1] + later[1])


def block_positions(rows, tok_dev, n_ctx):
    half = tok_dev // 2
    device = rows // tok_dev
    within = rows % tok_dev
    block = jnp.where(within < half, device, 2 * n_ctx - 1 - device)
    return block * half + within % half


def split_product(form, wide, narrow):
    upper = wide.astype(jnp.bfloat16)
    lower = (wide - upper.astype(jnp.float32)).astype(jnp.bfloat16)
    first_term = jnp.einsum(form, upper, narrow, preferred_element_type=jnp.float32)
    return first_term + jnp.einsum(form, lower, narrow, preferred_element_type=jnp.float32)


def body(
    queries,
    key_heads,
    head_values,
    hidden,
    out_proj,
    norm_gain,
    x_proj,
    bc_proj,
    dt_proj,
    dt_bias,
    decay_log,
    skip_gain,
):
    tok_dev = queries.shape[0]
    half = tok_dev // 2
    n_ctx = lax.axis_size("ctx")
    n_tp = lax.axis_size("tp")
    ctx_index = lax.axis_index("ctx")
    tp_index = lax.axis_index("tp")
    head_dim = key_heads.shape[2]
    kv_total = key_heads.shape[1]
    q_local = queries.shape[1] // head_dim
    group = q_local * n_tp // kv_total
    kv_local = max(1, q_local // group)
    per_kv = q_local // kv_local
    kv_start = tp_index * q_local // group
    keys_mine = lax.dynamic_slice_in_dim(key_heads, kv_start, kv_local, 1)
    values_mine = lax.dynamic_slice_in_dim(head_values, kv_start, kv_local, 1)
    query_pos = block_positions(
        ctx_index * tok_dev + jnp.arange(tok_dev, dtype=jnp.int32), tok_dev, n_ctx
    )
    shaped_q = queries.reshape(tok_dev, kv_local, per_kv, head_dim)
    root_dim = math.sqrt(head_dim)
    start_max = jnp.full((kv_local, per_kv, tok_dev), -1e30, jnp.float32)
    run_max = start_max
    key_piece = lax.all_gather(keys_mine, "ctx", axis=0, tiled=True)
    value_piece = lax.all_gather(values_mine, "ctx", axis=0, tiled=True)
    count = key_piece.shape[0]
    key_pos = block_positions(jnp.arange(count, dtype=jnp.int32), tok_dev, n_ctx)
    scores = (
        jnp.einsum("qgjd,kgd->gjqk", shaped_q, key_piece, preferred_element_type=jnp.float32)
        / root_dim
    )
    allowed = key_pos[None, :] <= query_pos[:, None]
    piece_max = jnp.max(jnp.where(allowed, scores, -1e30), axis=-1)
    new_max = jnp.maximum(run_max, piece_max)
    weights = jnp.where(allowed, jnp.exp(scores - new_max[..., None]), 0.0)
    run_sum = jnp.sum(weights, axis=-1)
    update = jnp.einsum(
        "gjqk,kgd->gjqd",
        weights.astype(jnp.bfloat16),
        value_piece,
        preferred_element_type=jnp.float32,
    )
    accum = update
    run_max, run_sum, accum = (new_max, run_sum, accum)
    attended = (
        jnp.transpose(accum / run_sum[..., None], (2, 0, 1, 3))
        .reshape(tok_dev, q_local * head_dim)
        .astype(jnp.bfloat16)
    )
    head_part = jnp.dot(attended, out_proj, preferred_element_type=jnp.float32)
    slice_width = hidden.shape[1] // n_tp
    attention_sum = lax.psum(head_part.astype(jnp.bfloat16), "tp").astype(jnp.float32)
    residual = (hidden.astype(jnp.float32) + attention_sum).astype(jnp.bfloat16)
    residual_out = lax.dynamic_slice_in_dim(residual, tp_index * slice_width, slice_width, 1)
    as_float = residual.astype(jnp.float32)
    mean_square = jnp.mean(as_float * as_float, axis=-1, keepdims=True)
    normed = (as_float * lax.rsqrt(mean_square + 1e-05) * norm_gain).astype(jnp.bfloat16)
    m_local = skip_gain.shape[0]
    state_size = bc_proj.shape[2] // 2
    groups_all = bc_proj.shape[1]
    per_group = m_local * n_tp // groups_all
    g_local = max(1, m_local // per_group)
    heads_each = m_local // g_local
    g_start = tp_index * m_local // per_group
    head_width = x_proj.shape[1] // m_local
    bc_mine = lax.dynamic_slice_in_dim(bc_proj, g_start, g_local, 1).reshape(
        bc_proj.shape[0], g_local * 2 * state_size
    )
    sum_x = jnp.dot(
        normed,
        lax.all_gather(x_proj, "ctx", axis=0, tiled=True),
        preferred_element_type=jnp.float32,
    )
    sum_bc = jnp.dot(
        normed,
        lax.all_gather(bc_mine, "ctx", axis=0, tiled=True),
        preferred_element_type=jnp.float32,
    )
    sum_dt = jnp.dot(
        normed,
        lax.all_gather(dt_proj, "ctx", axis=0, tiled=True),
        preferred_element_type=jnp.float32,
    )
    inputs_low = sum_x.astype(jnp.bfloat16).reshape(2, half, g_local, heads_each, head_width)
    inputs = inputs_low.astype(jnp.float32)
    bc_round = sum_bc.astype(jnp.bfloat16).reshape(2, half, g_local, 2 * state_size)
    b_low = bc_round[..., :state_size]
    c_low = bc_round[..., state_size:]
    steps = jax.nn.softplus(sum_dt + dt_bias).reshape(2, half, g_local, heads_each)
    rates = -jnp.exp(decay_log).reshape(g_local, heads_each)
    cumul = jnp.transpose(jnp.cumsum(steps * rates, axis=1), (0, 2, 3, 1))
    step_rows = jnp.transpose(steps, (0, 2, 3, 1))
    gram = jnp.einsum("ckgn,csgn->cgks", c_low, b_low, preferred_element_type=jnp.float32)
    places = jnp.arange(half, dtype=jnp.int32)
    causal = places[None, :] <= places[:, None]
    gaps = cumul[..., :, None] - cumul[..., None, :]
    decay = jnp.where(causal, jnp.exp(jnp.where(causal, gaps, 0.0)), 0.0)
    mixing = gram[:, :, None] * decay * step_rows[..., None, :]
    inner = split_product("cgjks,csgjp->ckgjp", mixing, inputs_low)
    last = cumul[..., -1]
    tail = jnp.exp(last[..., None] - cumul) * step_rows
    weighted = jnp.transpose(tail, (0, 3, 1, 2))[..., None] * inputs
    block_state = split_product("csgjp,csgn->cgjpn", weighted, b_low)
    block_decay = jnp.exp(last)
    first = (block_decay[0], block_state[0])
    second = (block_decay[1], block_state[1])
    unit = (jnp.ones_like(first[0]), jnp.zeros_like(first[1]))
    before = prefix(first, "ctx", chain, unit, False)
    last_device = ctx_index == n_ctx - 1
    through = chain(before, first)
    joined = chain(through, second)
    sent = (
        jnp.where(last_device, joined[0], second[0]),
        jnp.where(last_device, joined[1], second[1]),
    )
    after = prefix(sent, "ctx", chain, unit, True)
    second_in = jnp.where(last_device, through[1], after[1])
    entering = jnp.stack([before[1], second_in])
    carried = jnp.transpose(jnp.exp(cumul), (0, 3, 1, 2))[..., None] * split_product(
        "cgjpn,ckgn->ckgjp", entering, c_low
    )
    output = inner + carried + skip_gain.reshape(g_local, heads_each)[:, :, None] * inputs
    mamba_out = output.reshape(tok_dev, m_local * head_width).astype(jnp.bfloat16)
    return (residual_out, mamba_out)


def solution(mesh):
    placed = (
        P("ctx", "tp"),
        P("ctx", None, None),
        P("ctx", None, None),
        P("ctx", None),
        P("tp", None),
        P(),
        P("ctx", "tp"),
        P("ctx", None, None),
        P("ctx", "tp"),
        P("tp"),
        P("tp"),
        P("tp"),
    )
    return jax.shard_map(
        body,
        mesh=mesh,
        in_specs=placed,
        out_specs=(P("ctx", "tp"), P("ctx", "tp")),
        check_vma=False,
    )
```

profile of v0, /device:TPU:1, one launch (start us, length us, event | category | flops | bytes accessed | tf_op | source)
XLA Modules:
  0.0 671.6 jit_solution(12906673132283992635)
XLA Ops:
  7.2 1.2 constant_dynamic-slice_fusion.4
  9.1 1.1 constant_dynamic-slice_fusion.3
  11.0 66.9 %all-gather.13.cloned.1.call-done = bf16[8192,1,128]{2,0,1:T(8,128)(2,1)} async-done(((bf16[256,1,128]{2,0,1:T(8,128)(2,1)}), bf16[8192,1,128]{2,0,1:T(8,128)(2,1)}) %all-gather.13.cloned.1.call-update) | async-done | bytes 2097168 | tf_op jit(solution)/shard_map/all_gather | solution.py:80
  77.9 5.7 fusion.4
  83.6 3.3 copy-done.1
  86.9 3.7 fusion.5
  90.7 48.6 %all-gather.15.cloned.1.call-done = bf16[8192,1,128]{2,0,1:T(8,128)(2,1)} async-done(((bf16[256,1,128]{2,0,1:T(8,128)(2,1)}), bf16[8192,1,128]{2,0,1:T(8,128)(2,1)}) %all-gather.15.cloned.1.call-update) | async-done | bytes 2097168 | tf_op jit(solution)/shard_map/all_gather | solution.py:81
  139.3 8.7 %convolution_convert_fusion = bf16[256,4096]{1,0:T(8,128)(2,1)} fusion(bf16[128,4096]{1,0:T(8,128)(2,1)S(1)} %copy-done, bf16[8192,1,128]{2,0,1:T(8,128)(2,1)} %all-gather.15.cloned.1.call-done, f32[1,1,256,8192]{2,3,1,0:T(8,128)} %copy-done.1, f32[256]{0:T(256)S(1)} %broadcast_maximum_fusion, s32[256]{0:T(256)S(1)} %fusion.88, s32[8192]{0:T(1024)S(1)} %fusion.83, ...), kind=kOutput, calls=%fused_computation.18 | convolution fusion | flops 814809088 | bytes 13667328 | tf_op jit(solution)/shard_map/dot_general | solution.py:106
  149.5 43.0 %all_gather.37 = bf16[4096,4]{0,1:T(4,128)(2,1)S(1)} all-gather(bf16[128,4]{0,1:T(4,128)(2,1)S(1)} %copy-done.14), channel_id=1, replica_groups=mesh['ctx'=32,'tp'=16] {'ctx'}, dimensions={0}, use_global_device_ids=true | all-gather | bytes 33792 | tf_op jit(solution)/shard_map/all_gather | solution.py:137
  192.5 94.5 %all-reduce.2.cloned.1.call-done = bf16[256,4096]{1,0:T(8,128)(2,1)} async-done(((bf16[256,4096]{1,0:T(8,128)(2,1)}), bf16[256,4096]{1,0:T(8,128)(2,1)}) %all-reduce.2.cloned.1.call-update) | async-done | bytes 2097168 | tf_op jit(solution)/shard_map/psum | solution.py:108
  287.0 3.2 fusion.7
  290.2 68.7 %all-gather.17.cloned.1.call-done = bf16[4096,256]{1,0:T(8,128)(2,1)} async-done(((bf16[128,256]{1,0:T(8,128)(2,1)}), bf16[4096,256]{1,0:T(8,128)(2,1)}) %all-gather.17.cloned.1.call-update) | async-done | bytes 2097168 | tf_op jit(solution)/shard_map/all_gather | solution.py:127
  358.9 2.4 convolution_convert_fusion.1
  362.1 1.1 copy.90
  365.1 55.0 %all-gather.19.cloned.1.call-done = bf16[4096,1,256]{2,0,1:T(8,128)(2,1)} async-done(((bf16[128,1,256]{2,0,1:T(8,128)(2,1)}), bf16[4096,1,256]{2,0,1:T(8,128)(2,1)}) %all-gather.19.cloned.1.call-update) | async-done | bytes 2097168 | tf_op jit(solution)/shard_map/all_gather | solution.py:132
  420.1 2.4 fusion.24
  423.1 1.1 convolution_add_fusion.1
  425.6 43.8 %all-gather.1 = f32[32,1,4,1]{2,3,1,0:T(1,128)} all-gather(f32[1,1,4,1]{2,3,1,0:T(1,128)S(1)} %get-tuple-element.328), channel_id=3, replica_groups=mesh['ctx'=32,'tp'=16] {'ctx'}, dimensions={0}, use_global_device_ids=true | all-gather | bytes 528 | tf_op jit(solution)/shard_map/all_gather | solution.py:10
  469.4 19.7 %all-gather.21.cloned.1.call-done = f32[32,4,64,128]{3,2,1,0:T(8,128)} async-done(((f32[1,4,64,128]{3,2,1,0:T(8,128)}), f32[32,4,64,128]{3,2,1,0:T(8,128)}) %all-gather.21.cloned.1.call-update) | async-done | bytes 4194320 | tf_op jit(solution)/shard_map/all_gather | solution.py:10
  489.1 70.9 %while.30 = (s32[]{:T(128)}, f32[1,4]{1,0:T(1,128)S(1)}, f32[1,4,64,128]{3,2,1,0:T(8,128)S(1)}, s32[]{:T(128)}, f32[32,1,4]{2,1,0:T(1,128)}, /*index=5*/f32[32,1,4,64,128]{4,3,2,1,0:T(8,128)}, s32[]{:T(128)}, s32[]{:T(128)}) while((s32[]{:T(128)}, f32[1,4]{1,0:T(1,128)S(1)}, f32[1,4,64,128]{3,2,1,0:T(8,128)S(1)}, s32[]{:T(128)}, ...), condition=%wide.region_6.7_spmd.clone, body=%wide.region_5.6_spmd.clone.sunk | while | flops 131088 | bytes 393431 | solution.py:22
  560.0 1.3 add_select_fusion
  561.4 2.0 reshape.405
  564.3 2.0 copy.102
  567.0 1.0 fusion.65
  568.0 1.3 fusion.50
  570.0 42.2 %all-gather.5 = f32[32,1,4]{2,1,0:T(1,128)S(1)} all-gather(f32[1,1,4]{2,1,0:T(1,128)S(1)} %fusion.91), channel_id=5, replica_groups=mesh['ctx'=32,'tp'=16] {'ctx'}, dimensions={0}, use_global_device_ids=true | all-gather | bytes 528 | tf_op jit(solution)/shard_map/all_gather | solution.py:10
  612.5 13.4 %all-gather.23.cloned.1.call-done = f32[32,4,64,128]{3,2,1,0:T(8,128)} async-done(((f32[1,4,64,128]{3,2,1,0:T(8,128)}), f32[32,4,64,128]{3,2,1,0:T(8,128)}) %all-gather.23.cloned.1.call-update) | async-done | bytes 4194320 | tf_op jit(solution)/shard_map/all_gather | solution.py:10
  625.9 4.8 reverse_bitcast_fusion
  630.7 32.0 %while.31 = (s32[]{:T(128)}, f32[1,4,64,128]{3,2,1,0:T(8,128)S(1)}, s32[]{:T(128)}, f32[32,1,4]{2,1,0:T(1,128)S(1)}, f32[32,1,4,64,128]{4,3,2,1,0:T(8,128)}, /*index=5*/s32[]{:T(128)}, s32[]{:T(128)}) while((s32[]{:T(128)}, f32[1,4,64,128]{3,2,1,0:T(8,128)S(1)}, s32[]{:T(128)}, f32[32,1,4]{2,1,0:T(1,128)S(1)}, ...), condition=%wide.region_8.9_spmd.clone, body=%wide.region_7.8_spmd.clone.sunk | while | flops 131076 | bytes 393369 | solution.py:22
  631.8 1.0 fusion.113
  632.8 1.0 fusion.113
  633.8 1.0 fusion.113
  634.9 1.0 fusion.113
  636.9 1.0 fusion.113
  638.0 1.0 fusion.113
  639.0 1.0 fusion.113
  640.0 1.0 fusion.113
  641.1 1.0 fusion.113
  642.1 1.0 fusion.113
  644.2 1.0 fusion.113
  645.2 1.0 fusion.113
  646.2 1.0 fusion.113
  647.3 1.0 fusion.113
  648.3 1.0 fusion.113
  649.3 1.0 fusion.113
  650.4 1.0 fusion.113
  651.4 1.0 fusion.113
  652.4 1.0 fusion.113
  (226 shorter events, 95.0 us)
Async XLA Ops:
  7.2 132.1 %copy-start = (bf16[128,4096]{1,0:T(8,128)(2,1)S(1)}, bf16[128,4096]{1,0:T(8,128)(2,1)}, u32[]{:S(2)}) copy-start(bf16[128,4096]{1,0:T(8,128)(2,1)} %param.20) | copy-start | bytes 3145732
  7.2 70.7 %all-gather.13.cloned.1.call-start = ((), (), s32[]{:S(2)}) async-start(), calls=%async_computation | async-start | bytes 2162688 | tf_op jit(solution)/shard_map/all_gather | solution.py:80
  9.1 130.2 %all-gather.15.cloned.1.call-start = ((), (), s32[]{:S(2)}) async-start(), calls=%async_computation.1 | async-start | bytes 2162688 | tf_op jit(solution)/shard_map/all_gather | solution.py:81
  10.9 276.1 %all-reduce.2.cloned.1.call-start = ((), (), s32[]{:S(2)}) async-start(), calls=%async_computation.2 | async-start | bytes 4194304 | tf_op jit(solution)/shard_map/psum | solution.py:108
  83.6 3.3 copy-start.1
  90.6 58.0 %copy-start.11 = (bf16[128,4,256]{2,1,0:T(4,128)(2,1)S(1)}, bf16[128,4,256]{2,1,0:T(4,128)(2,1)}, u32[]{:S(2)}) copy-start(bf16[128,4,256]{2,1,0:T(4,128)(2,1)} %param.23) | copy-start | bytes 786436
  90.6 58.9 %copy-start.14 = (bf16[128,4]{0,1:T(4,128)(2,1)S(1)}, bf16[128,4]{0,1:T(4,128)(2,1)}, u32[]{:S(2)}) copy-start(bf16[128,4]{0,1:T(4,128)(2,1)} %param.24) | copy-start | bytes 3076
  90.6 101.8 %copy-start.17 = (f32[4]{0:T(128)S(1)}, f32[4]{0:T(128)}, u32[]{:S(2)}) copy-start(f32[4]{0:T(128)} %param.26) | copy-start | bytes 52
  148.0 210.9 %copy-start.16 = (f32[4096]{0:T(1024)S(1)}, f32[4096]{0:T(1024)}, u32[]{:S(2)}) copy-start(f32[4096]{0:T(1024)} %param.21) | copy-start | bytes 49156
  148.0 210.9 %all-gather.17.cloned.1.call-start = ((), (), s32[]{:S(2)}) async-start(), calls=%async_computation.3 | async-start | bytes 2162688 | tf_op jit(solution)/shard_map/all_gather | solution.py:127
  148.6 271.5 %all-gather.19.cloned.1.call-start = ((), (), s32[]{:S(2)}) async-start(), calls=%async_computation.4 | async-start | bytes 2162688 | tf_op jit(solution)/shard_map/all_gather | solution.py:132
  149.4 339.7 %all-gather.21.cloned.1.call-start = ((), (), s32[]{:S(2)}) async-start(), calls=%async_computation.5 | async-start | bytes 4325376 | tf_op jit(solution)/shard_map/all_gather | solution.py:10
  290.2 73.0 %copy-start.18 = (f32[4]{0:T(128)S(1)}, f32[4]{0:T(128)}, u32[]{:S(2)}) copy-start(f32[4]{0:T(128)} %param.25) | copy-start | bytes 52
  290.2 73.8 %copy-start.15 = (f32[256]{0:T(256)}, f32[256]{0:T(256)S(1)}, u32[]{:S(2)}) copy-start(f32[256]{0:T(256)S(1)} %add_rsqrt_fusion) | copy-start | bytes 3076
  361.3 2.8 copy-start.9
  363.2 59.3 %copy-start.5 = (bf16[2,128,4,64]{1,3,2,0:T(8,128)(2,1)}, bf16[2,128,4,64]{1,3,2,0:T(8,128)(2,1)S(1)}, u32[]{:S(2)}) copy-start(bf16[2,128,4,64]{1,3,2,0:T(8,128)(2,1)S(1)} %copy.90) | copy-start | bytes 393220
  364.3 60.6 %copy-start.4 = (f32[2,128,1,4]{3,2,1,0:T(1,128)}, f32[2,128,1,4]{3,2,1,0:T(1,128)S(1)}, u32[]{:S(2)}) copy-start(f32[2,128,1,4]{3,2,1,0:T(1,128)S(1)} %fusion.59) | copy-start | bytes 12292
  365.1 60.0 %copy-start.12 = (f32[2,1,4,1]{2,1,3,0:T(1,128)S(1)}, f32[2,1,4,1]{2,1,3,0:T(1,128)}, u32[]{:S(2)}) copy-start(f32[2,1,4,1]{2,1,3,0:T(1,128)} %get-tuple-element.323) | copy-start | bytes 100
  422.5 0.7 copy-start.7
  424.2 137.1 %copy-start.2 = (f32[2,4,64,128]{3,2,1,0:T(8,128)}, f32[2,4,64,128]{3,2,1,0:T(8,128)S(1)}, u32[]{:S(2)}) copy-start(f32[2,4,64,128]{3,2,1,0:T(8,128)S(1)} %convolution_add_fusion.1) | copy-start | bytes 786436
  425.0 201.0 %all-gather.23.cloned.1.call-start = ((), (), s32[]{:S(2)}) async-start(), calls=%async_computation.6 | async-start | bytes 4325376 | tf_op jit(solution)/shard_map/all_gather | solution.py:10
  612.5 50.3 %copy-start.3 = (f32[2,4,64,128]{3,2,1,0:T(8,128)S(1)}, f32[2,4,64,128]{3,2,1,0:T(8,128)}, u32[]{:S(2)}) copy-start(f32[2,4,64,128]{3,2,1,0:T(8,128)} %copy-done.2) | copy-start | bytes 786436
  612.5 50.3 %copy-start.13 = (f32[4]{0:T(128)S(1)}, f32[4]{0:T(128)}, u32[]{:S(2)}) copy-start(f32[4]{0:T(128)} %get-tuple-element.326) | copy-start | bytes 52
  612.5 50.4 %copy-start.8 = (bf16[256,256]{1,0:T(8,128)(2,1)S(1)}, bf16[256,256]{1,0:T(8,128)(2,1)}, u32[]{:S(2)}) copy-start(bf16[256,256]{1,0:T(8,128)(2,1)} %copy-done.7) | copy-start | bytes 393220
  612.5 50.8 %copy-start.6 = (bf16[2,128,4,64]{1,3,2,0:T(8,128)(2,1)S(1)}, bf16[2,128,4,64]{1,3,2,0:T(8,128)(2,1)}, u32[]{:S(2)}) copy-start(bf16[2,128,4,64]{1,3,2,0:T(8,128)(2,1)} %copy-done.5) | copy-start | bytes 393220
  612.5 50.8 %copy-start.10 = (f32[2,128,1,4,64]{1,4,3,0,2:T(8,128)S(1)}, f32[2,128,1,4,64]{1,4,3,0,2:T(8,128)}, u32[]{:S(2)}) copy-start(f32[2,128,1,4,64]{1,4,3,0,2:T(8,128)} %copy.102) | copy-start | bytes 786436
  612.5 50.8 %copy-start.19 = (f32[4]{0:T(128)S(1)}, f32[4]{0:T(128)}, u32[]{:S(2)}) copy-start(f32[4]{0:T(128)} %param.27) | copy-start | bytes 52
Sparse Core Ops, SparseCore 0:
  11.7 66.1 all-gather.12
  81.6 57.6 all-gather.14
  148.1 138.8 all-reduce.1
  290.0 68.8 all-gather.16
  362.4 57.6 all-gather.18
  425.1 63.9 all-gather.20
  561.5 64.4 all-gather.22
where the time goes:
time: 674 us; the launch traced here: 672 us
  waiting for transfers between devices  368 us (55%)
  blocking collectives  129 us (19%)
  other arithmetic  91 us (14%)
  local copies, waits for them, and re-layouts  43.9 us (7%)
  matrix products  24.1 us (4%)
  between operations  14.6 us (2%)
    psum x1, waiting for transfers between devices, body(): lax.psum(head_part.astype(jnp.bfloat16), 'tp').astype(jnp.float32)  94.5 us
    all_gather x2, blocking collectives, prefix(): pieces = jax.tree.map(lambda part: lax.all_gather(part, axis), value)  86.1 us
    select_n x93, other arithmetic, lap(): jnp.where(position < mine, new, old)  81.7 us
    all_gather x1, waiting for transfers between devices, body(): lax.all_gather(x_proj, 'ctx', axis=0, tiled=True)  68.7 us
    all_gather x1, waiting for transfers between devices, body(): key_piece = lax.all_gather(keys_mine, 'ctx', axis=0, tiled=True)  66.9 us
    all_gather x1, waiting for transfers between devices, body(): lax.all_gather(bc_mine, 'ctx', axis=0, tiled=True)  55 us
    all_gather x1, waiting for transfers between devices, body(): value_piece = lax.all_gather(values_mine, 'ctx', axis=0, tiled=True)  48.6 us
    all_gather x1, blocking collectives, body(): lax.all_gather(dt_proj, 'ctx', axis=0, tiled=True)  43 us
  transfers between devices with their start and end apart: 7, of which 7 were waited for; matrix products, arithmetic and copies ran while one was open for 5% of the time, Pallas kernels for 0%

commit v1 on v0

--- a/solution.py
+++ b/solution.py
@@ -3,6 +3,10 @@
 import jax.numpy as jnp
 from jax import lax
 from jax.sharding import PartitionSpec as P
+
+
+def view_goods(xs, device_axis):
+    return jnp.sum(lax.all_gather(xs, device_axis), 0)
 
 
 def prefix(value, axis, join, neutral, backward):
@@ -105,7 +109,7 @@
     )
     head_part = jnp.dot(attended, out_proj, preferred_element_type=jnp.float32)
     slice_width = hidden.shape[1] // n_tp
-    attention_sum = lax.psum(head_part.astype(jnp.bfloat16), "tp").astype(jnp.float32)
+    attention_sum = view_goods(head_part.astype(jnp.bfloat16), "tp").astype(jnp.float32)
     residual = (hidden.astype(jnp.float32) + attention_sum).astype(jnp.bfloat16)
     residual_out = lax.dynamic_slice_in_dim(residual, tp_index * slice_width, slice_width, 1)
     as_float = residual.astype(jnp.float32)

time: 674 us -> 1170 us (1.74)
  waiting for transfers between devices: 368 us -> 880 us
  local copies, waits for them, and re-layouts: 43.9 us -> 18.9 us
  blocking collectives: 129 us -> 151 us
    all_gather x0 -> x1, waiting for transfers between devices: none -> 621 us  [view_goods(): return jnp.sum(lax.all_gather(xs, device_axis), 0)]
    psum x1 -> x0, waiting for transfers between devices: 94.5 us -> none  [body(): lax.psum(head_part.astype(jnp.bfloat16), 'tp').astype(jnp.float32)]
    all_gather x1, blocking collectives: 43 us -> 66.3 us  [body(): lax.all_gather(dt_proj, 'ctx', axis=0, tiled=True)]
    all_gather x1, waiting for transfers between devices: 68.7 us -> 48.4 us  [body(): lax.all_gather(x_proj, 'ctx', axis=0, tiled=True)]
    mul x63, local copies, waits for them, and re-layouts: 20.6 us -> 0.42 us  [chain(): later[0][..., None, None] * earlier[1] + later[1]]
    select_n x93, other arithmetic: 81.7 us -> 62.1 us  [lap(): jnp.where(position < mine, new, old)]
  transfers between devices with their start and end apart: 7 -> 7, of which waited for: 7 -> 7; matrix products, arithmetic and copies ran while one was open for 5% -> 3% of each run, Pallas kernels for 0% -> 0%
where the time goes in v1:
time: 1170 us
  waiting for transfers between devices  880 us (75%)
  blocking collectives  151 us (13%)
  other arithmetic  83.1 us (7%)
  matrix products  22.8 us (2%)
  local copies, waits for them, and re-layouts  18.9 us (2%)
  between operations  14.6 us (1%)
    all_gather x1, waiting for transfers between devices, view_goods(): return jnp.sum(lax.all_gather(xs, device_axis), 0)  621 us
    all_gather x2, blocking collectives, prefix(): pieces = jax.tree.map(lambda part: lax.all_gather(part, axis), value)  84.5 us
    all_gather x1, waiting for transfers between devices, body(): key_piece = lax.all_gather(keys_mine, 'ctx', axis=0, tiled=True)  66.9 us
    all_gather x1, blocking collectives, body(): lax.all_gather(dt_proj, 'ctx', axis=0, tiled=True)  66.3 us
    select_n x93, other arithmetic, lap(): jnp.where(position < mine, new, old)  62.1 us
    all_gather x1, waiting for transfers between devices, body(): lax.all_gather(bc_mine, 'ctx', axis=0, tiled=True)  56.7 us
    all_gather x1, waiting for transfers between devices, body(): value_piece = lax.all_gather(values_mine, 'ctx', axis=0, tiled=True)  48.7 us
    all_gather x1, waiting for transfers between devices, body(): lax.all_gather(x_proj, 'ctx', axis=0, tiled=True)  48.4 us
  transfers between devices with their start and end apart: 7, of which 7 were waited for; matrix products, arithmetic and copies ran while one was open for 3% of the time, Pallas kernels for 0%

profile of v1, /device:TPU:1, one launch (start us, length us, event | category | flops | bytes accessed | tf_op | source)
XLA Modules:
  0.0 1172.8 jit_solution(13169927894742688786)
XLA Ops:
  7.2 1.2 constant_dynamic-slice_fusion.4
  9.1 1.1 constant_dynamic-slice_fusion.3
  11.0 66.9 %all-gather.15.cloned.1.call-done = bf16[8192,1,128]{2,0,1:T(8,128)(2,1)} async-done(((bf16[256,1,128]{2,0,1:T(8,128)(2,1)}), bf16[8192,1,128]{2,0,1:T(8,128)(2,1)}) %all-gather.15.cloned.1.call-update) | async-done | bytes 2097168 | tf_op jit(solution)/shard_map/all_gather | solution.py:84
  77.9 5.7 fusion.4
  83.6 3.2 copy-done.2
  86.9 3.7 fusion.5
  90.6 48.7 %all-gather.17.cloned.1.call-done = bf16[8192,1,128]{2,0,1:T(8,128)(2,1)} async-done(((bf16[256,1,128]{2,0,1:T(8,128)(2,1)}), bf16[8192,1,128]{2,0,1:T(8,128)(2,1)}) %all-gather.17.cloned.1.call-update) | async-done | bytes 2097168 | tf_op jit(solution)/shard_map/all_gather | solution.py:85
  139.3 8.6 convolution_convert_fusion
  149.5 66.3 %all_gather.45 = bf16[4096,4]{0,1:T(4,128)(2,1)S(1)} all-gather(bf16[128,4]{0,1:T(4,128)(2,1)S(1)} %copy-done.17), channel_id=1, replica_groups=mesh['ctx'=32,'tp'=16] {'ctx'}, dimensions={0}, use_global_device_ids=true | all-gather | bytes 33792 | tf_op jit(solution)/shard_map/all_gather | solution.py:141
  215.8 620.6 %all-gather.21.cloned.1.call-done = bf16[4096,4096]{1,0:T(8,128)(2,1)} async-done(((bf16[256,4096]{1,0:T(8,128)(2,1)}), bf16[4096,4096]{1,0:T(8,128)(2,1)}) %all-gather.21.cloned.1.call-update) | async-done | bytes 33554448 | tf_op jit(solution)/shard_map/all_gather | solution.py:9
  836.3 11.7 reduce_sum.31
  848.0 3.9 fusion.7
  851.9 48.4 %all-gather.19.cloned.1.call-done = bf16[4096,256]{1,0:T(8,128)(2,1)} async-done(((bf16[128,256]{1,0:T(8,128)(2,1)}), bf16[4096,256]{1,0:T(8,128)(2,1)}) %all-gather.19.cloned.1.call-update) | async-done | bytes 2097168 | tf_op jit(solution)/shard_map/all_gather | solution.py:131
  900.4 3.0 convolution_convert_fusion.1
  904.9 56.7 %all-gather.23.cloned.1.call-done = bf16[4096,1,256]{2,0,1:T(8,128)(2,1)} async-done(((bf16[128,1,256]{2,0,1:T(8,128)(2,1)}), bf16[4096,1,256]{2,0,1:T(8,128)(2,1)}) %all-gather.23.cloned.1.call-update) | async-done | bytes 2097168 | tf_op jit(solution)/shard_map/all_gather | solution.py:136
  961.6 2.4 fusion.24
  965.2 42.3 %all-gather.2 = f32[32,1,4,1]{2,3,1,0:T(1,128)S(1)} all-gather(f32[1,1,4,1]{2,3,1,0:T(1,128)S(1)} %get-tuple-element.328), channel_id=4, replica_groups=mesh['ctx'=32,'tp'=16] {'ctx'}, dimensions={0}, use_global_device_ids=true | all-gather | bytes 528 | tf_op jit(solution)/shard_map/all_gather | solution.py:14
  1007.4 21.7 %all-gather.25.cloned.1.call-done = f32[32,4,64,128]{3,2,1,0:T(8,128)} async-done(((f32[1,4,64,128]{3,2,1,0:T(8,128)}), f32[32,4,64,128]{3,2,1,0:T(8,128)}) %all-gather.25.cloned.1.call-update) | async-done | bytes 4194320 | tf_op jit(solution)/shard_map/all_gather | solution.py:14
  1029.1 32.6 %while.30 = (s32[]{:T(128)}, f32[1,4]{1,0:T(1,128)S(1)}, f32[1,4,64,128]{3,2,1,0:T(8,128)S(1)}, s32[]{:T(128)}, f32[32,1,4]{2,1,0:T(1,128)S(1)}, /*index=5*/f32[32,1,4,64,128]{4,3,2,1,0:T(8,128)}, s32[]{:T(128)}, s32[]{:T(128)}) while((s32[]{:T(128)}, f32[1,4]{1,0:T(1,128)S(1)}, f32[1,4,64,128]{3,2,1,0:T(8,128)S(1)}, s32[]{:T(128)}, ...), condition=%wide.region_6.7_spmd.clone, body=%wide.region_5.6_spmd.clone.sunk | while | flops 131088 | bytes 393431 | solution.py:26
  1031.3 1.0 fusion.112
  1032.3 1.0 fusion.112
  1035.5 1.0 fusion.112
  1036.5 1.0 fusion.112
  1038.6 1.0 fusion.112
  1039.7 1.0 fusion.112
  1040.7 1.0 fusion.112
  1042.8 1.0 fusion.112
  1043.9 1.0 fusion.112
  1047.0 1.0 fusion.112
  1048.1 1.0 fusion.112
  1051.2 1.0 fusion.112
  1052.3 1.0 fusion.112
  1055.5 1.0 fusion.112
  1056.5 1.0 fusion.112
  1058.6 1.0 fusion.112
  1059.7 1.0 fusion.112
  1060.7 1.0 fusion.112
  1063.1 1.2 reshape.406
  1066.7 1.1 fusion.50
  1067.9 42.2 %all-gather.6 = f32[32,1,4]{2,1,0:T(1,128)S(1)} all-gather(f32[1,1,4]{2,1,0:T(1,128)S(1)} %fusion.91), channel_id=6, replica_groups=mesh['ctx'=32,'tp'=16] {'ctx'}, dimensions={0}, use_global_device_ids=true | all-gather | bytes 528 | tf_op jit(solution)/shard_map/all_gather | solution.py:14
  1110.4 16.7 %all-gather.27.cloned.1.call-done = f32[32,4,64,128]{3,2,1,0:T(8,128)} async-done(((f32[1,4,64,128]{3,2,1,0:T(8,128)}), f32[32,4,64,128]{3,2,1,0:T(8,128)}) %all-gather.27.cloned.1.call-update) | async-done | bytes 4194320 | tf_op jit(solution)/shard_map/all_gather | solution.py:14
  1127.1 4.8 reverse_bitcast_fusion
  1132.0 32.0 %while.31 = (s32[]{:T(128)}, f32[1,4,64,128]{3,2,1,0:T(8,128)S(1)}, s32[]{:T(128)}, f32[32,1,4]{2,1,0:T(1,128)S(1)}, f32[32,1,4,64,128]{4,3,2,1,0:T(8,128)}, /*index=5*/s32[]{:T(128)}, s32[]{:T(128)}) while((s32[]{:T(128)}, f32[1,4,64,128]{3,2,1,0:T(8,128)S(1)}, s32[]{:T(128)}, f32[32,1,4]{2,1,0:T(1,128)S(1)}, ...), condition=%wide.region_8.9_spmd.clone, body=%wide.region_7.8_spmd.clone.sunk | while | flops 131076 | bytes 393369 | solution.py:26
  1134.0 1.0 fusion.113
  1135.1 1.0 fusion.113
  1137.1 1.0 fusion.113
  1138.1 1.0 fusion.113
  1139.2 1.0 fusion.113
  (231 shorter events, 51.3 us)
Async XLA Ops:
  7.2 132.1 %copy-start = (bf16[128,4096]{1,0:T(8,128)(2,1)S(1)}, bf16[128,4096]{1,0:T(8,128)(2,1)}, u32[]{:S(2)}) copy-start(bf16[128,4096]{1,0:T(8,128)(2,1)} %param.20) | copy-start | bytes 3145732
  7.2 70.7 %all-gather.15.cloned.1.call-start = ((), (), s32[]{:S(2)}) async-start(), calls=%async_computation | async-start | bytes 2162688 | tf_op jit(solution)/shard_map/all_gather | solution.py:84
  9.1 130.2 %all-gather.17.cloned.1.call-start = ((), (), s32[]{:S(2)}) async-start(), calls=%async_computation.1 | async-start | bytes 2162688 | tf_op jit(solution)/shard_map/all_gather | solution.py:85
  10.9 825.4 %all-gather.21.cloned.1.call-start = ((), (), s32[]{:S(2)}) async-start(), calls=%async_computation.3 | async-start | bytes 35651584 | tf_op jit(solution)/shard_map/all_gather | solution.py:9
  83.6 3.3 copy-start.2
  90.6 58.0 %copy-start.10 = (bf16[128,4,256]{2,1,0:T(4,128)(2,1)S(1)}, bf16[128,4,256]{2,1,0:T(4,128)(2,1)}, u32[]{:S(2)}) copy-start(bf16[128,4,256]{2,1,0:T(4,128)(2,1)} %param.23) | copy-start | bytes 786436
  90.6 58.9 %copy-start.17 = (bf16[128,4]{0,1:T(4,128)(2,1)S(1)}, bf16[128,4]{0,1:T(4,128)(2,1)}, u32[]{:S(2)}) copy-start(bf16[128,4]{0,1:T(4,128)(2,1)} %param.24) | copy-start | bytes 3076
  90.6 125.2 %copy-start.19 = (f32[4]{0:T(128)S(1)}, f32[4]{0:T(128)}, u32[]{:S(2)}) copy-start(f32[4]{0:T(128)} %param.26) | copy-start | bytes 52
  148.0 752.4 %all-gather.19.cloned.1.call-start = ((), (), s32[]{:S(2)}) async-start(), calls=%async_computation.2 | async-start | bytes 2162688 | tf_op jit(solution)/shard_map/all_gather | solution.py:131
  148.5 813.0 %all-gather.23.cloned.1.call-start = ((), (), s32[]{:S(2)}) async-start(), calls=%async_computation.4 | async-start | bytes 2162688 | tf_op jit(solution)/shard_map/all_gather | solution.py:136
  149.4 879.7 %all-gather.25.cloned.1.call-start = ((), (), s32[]{:S(2)}) async-start(), calls=%async_computation.5 | async-start | bytes 4325376 | tf_op jit(solution)/shard_map/all_gather | solution.py:14
  848.0 52.4 %copy-start.18 = (f32[4096]{0:T(1024)S(1)}, f32[4096]{0:T(1024)}, u32[]{:S(2)}) copy-start(f32[4096]{0:T(1024)} %param.21) | copy-start | bytes 49156
  851.9 51.8 %copy-start.3 = (bf16[256,4096]{1,0:T(8,128)(2,1)S(1)}, bf16[256,4096]{1,0:T(8,128)(2,1)}, u32[]{:S(2)}) copy-start(bf16[256,4096]{1,0:T(8,128)(2,1)} %get-tuple-element.321) | copy-start | bytes 6291460
  851.9 51.8 %copy-start.20 = (f32[4]{0:T(128)S(1)}, f32[4]{0:T(128)}, u32[]{:S(2)}) copy-start(f32[4]{0:T(128)} %param.25) | copy-start | bytes 52
  903.4 60.6 %copy-start.8 = (bf16[256,256]{1,0:T(8,128)(2,1)}, bf16[256,256]{1,0:T(8,128)(2,1)S(1)}, u32[]{:S(2)}) copy-start(bf16[256,256]{1,0:T(8,128)(2,1)S(1)} %convolution_convert_fusion.1) | copy-start | bytes 393220
  964.0 146.3 %copy-start.6 = (bf16[256,256]{1,0:T(8,128)(2,1)}, bf16[256,256]{1,0:T(8,128)(2,1)S(1)}, u32[]{:S(2)}) copy-start(bf16[256,256]{1,0:T(8,128)(2,1)S(1)} %fusion.24) | copy-start | bytes 393220
  964.3 102.3 %copy-start.4 = (f32[2,4,64,128]{3,2,1,0:T(8,128)}, f32[2,4,64,128]{3,2,1,0:T(8,128)S(1)}, u32[]{:S(2)}) copy-start(f32[2,4,64,128]{3,2,1,0:T(8,128)S(1)} %convolution_add_fusion.1) | copy-start | bytes 786436
  965.1 162.1 %all-gather.27.cloned.1.call-start = ((), (), s32[]{:S(2)}) async-start(), calls=%async_computation.6 | async-start | bytes 4325376 | tf_op jit(solution)/shard_map/all_gather | solution.py:14
  965.1 97.4 %copy-start.12 = (f32[4]{0:T(128)}, f32[4]{0:T(128)S(1)}, u32[]{:S(2)}) copy-start(f32[4]{0:T(128)S(1)} %get-tuple-element.326) | copy-start | bytes 52
  1065.0 45.4 %copy-start.15 = (f32[2,4,128]{2,1,0:T(4,128)}, f32[2,4,128]{2,1,0:T(4,128)S(1)}, u32[]{:S(2)}) copy-start(f32[2,4,128]{2,1,0:T(4,128)S(1)} %copy.89) | copy-start | bytes 12292
  1110.4 53.6 %copy-start.5 = (f32[2,4,64,128]{3,2,1,0:T(8,128)S(1)}, f32[2,4,64,128]{3,2,1,0:T(8,128)}, u32[]{:S(2)}) copy-start(f32[2,4,64,128]{3,2,1,0:T(8,128)} %copy-done.4) | copy-start | bytes 786436
  1110.4 53.6 %copy-start.13 = (f32[4]{0:T(128)S(1)}, f32[4]{0:T(128)}, u32[]{:S(2)}) copy-start(f32[4]{0:T(128)} %copy-done.12) | copy-start | bytes 52
  1110.4 53.7 %copy-start.7 = (bf16[256,256]{1,0:T(8,128)(2,1)S(1)}, bf16[256,256]{1,0:T(8,128)(2,1)}, u32[]{:S(2)}) copy-start(bf16[256,256]{1,0:T(8,128)(2,1)} %copy-done.6) | copy-start | bytes 393220
  1110.4 54.0 %copy-start.9 = (f32[2,128,1,4,64]{1,4,3,0,2:T(8,128)S(1)}, f32[2,128,1,4,64]{1,4,3,0,2:T(8,128)}, u32[]{:S(2)}) copy-start(f32[2,128,1,4,64]{1,4,3,0,2:T(8,128)} %copy.102) | copy-start | bytes 786436
  1110.4 54.0 %copy-start.11 = (pred[128,128]{1,0:T(8,128)(4,1)S(1)}, pred[128,128]{1,0:T(8,128)(4,1)}, u32[]{:S(2)}) copy-start(pred[128,128]{1,0:T(8,128)(4,1)} %iota_compare_fusion) | copy-start | bytes 49156
  1110.4 54.0 %copy-start.14 = (f32[2,4,128]{2,1,0:T(4,128)S(1)}, f32[2,4,128]{2,1,0:T(4,128)}, u32[]{:S(2)}) copy-start(f32[2,4,128]{2,1,0:T(4,128)} %copy.87) | copy-start | bytes 12292
  1110.4 54.0 %copy-start.21 = (f32[4]{0:T(128)S(1)}, f32[4]{0:T(128)}, u32[]{:S(2)}) copy-start(f32[4]{0:T(128)} %param.27) | copy-start | bytes 52
  1127.1 37.4 %copy-start.16 = (f32[2,4,128]{2,1,0:T(4,128)S(1)}, f32[2,4,128]{2,1,0:T(4,128)}, u32[]{:S(2)}) copy-start(f32[2,4,128]{2,1,0:T(4,128)} %copy-done.15) | copy-start | bytes 12292
  1127.1 38.8 %copy-start.1 = (bf16[128,4096]{1,0:T(8,128)(2,1)S(1)}, bf16[128,4096]{1,0:T(8,128)(2,1)}, u32[]{:S(2)}) copy-start(bf16[128,4096]{1,0:T(8,128)(2,1)} %param.20) | copy-start | bytes 3145732
Sparse Core Ops, SparseCore 0:
  11.7 66.1 all-gather.14
  81.6 57.6 all-gather.16
  148.1 688.2 all-gather.20
  839.3 60.9 all-gather.18
  903.9 57.6 all-gather.22
  965.2 63.9 all-gather.24
  1062.6 64.4 all-gather.26
